TPU v7x, 512 devices: a whole 4x8x8 slice. The times are simulated.
512 devices in a mesh: req: 128 (over y, z, core), tp: 4 (over x).
Axes of the slice: x: 4, y: 8, z: 8, core: 2. Of those that a mesh axis runs over, the one named last changes fastest.
Arguments:
- attn_out: bfloat16 [8192, 2048], P('req', 'tp'), may hold values from -6 to 6
- w_out: bfloat16 [2048, 2048], P('tp'), may hold values from -0.125 to 0.125
- residual: bfloat16 [8192, 2048], P('req', 'tp'), may hold values from -6 to 6
- routes: int32 [8192, 6], P('req'), may hold values from 0 to 127, all different within a row; in each aligned block of 64 rows (0 to 63, 64 to 127, ...) at most 6 rows name the same one
- gates: float32 [8192, 6], P('req'), may hold values from 0.05 to 1
- w_gate: bfloat16 [128, 2048, 1024], P('req', None, 'tp'), as said below
- w_up: bfloat16 [128, 2048, 1024], P('req', None, 'tp'), as said below
- w_down: bfloat16 [128, 1024, 2048], P('req', None, 'tp'), as said below
- norm_gain: float32 [2048], P('tp'), may hold values from 0.1 to 1.9
Outputs:
- normed: bfloat16 [8192, 2048], P('req', 'tp')
Inputs may be any that keep to these rules, and one draw needn't show every extreme that they name: `routes`: each row names 6 different slots. In the 64 rows of one index of req no slot is named by more than 6 rows, a bound that some block reaches. `w_gate`: slots 2 e and 2 e + 1 hold the same expert e: their weights are equal. `w_up`: slots 2 e and 2 e + 1 hold the same expert e: their weights are equal. `w_down`: slots 2 e and 2 e + 1 hold the same expert e: their weights are equal.
All inputs are finite; a program needn't handle non-finite values.
Results may differ from a plain program's by a relative error of at most 0.0056.
Values may be sent and summed in bfloat16 or wider, within the bound.
A program may use at most 64 MiB of HBM per device.

v0:
```python
import jax
import jax.numpy as jnp
from jax import lax
from jax.sharding import PartitionSpec as P


def body(attn_out, w_out, residual, routes, gates, w_gate, w_up, w_down, norm_gain):
    row_count = attn_out.shape[0]
    part_width = residual.shape[1]
    full_width = w_out.shape[1]
    route_count = routes.shape[1]
    slot_count = lax.axis_size("req")
    capacity = max(2, min(row_count, 2 * row_count * route_count // slot_count))
    tp_index = lax.axis_index("tp")
    partial_value = jnp.dot(attn_out, w_out, preferred_element_type=jnp.float32)
    own_block = lax.dynamic_slice_in_dim(partial_value, tp_index * part_width, part_width, 1)
    partial_value = lax.dynamic_update_slice_in_dim(
        partial_value, own_block + residual.astype(jnp.float32), tp_index * part_width, 1
    )
    flat_routes = routes.reshape(-1)
    one_hot = (flat_routes[:, None] == jnp.arange(slot_count, dtype=jnp.int32)[None, :]).astype(
        jnp.int32
    )
    position = jnp.sum(one_hot * (jnp.cumsum(one_hot, axis=0) - 1), axis=1)
    dest_index = flat_routes * capacity + position
    row_ids = jnp.repeat(jnp.arange(row_count, dtype=jnp.int32), route_count)
    source_row = jnp.zeros((slot_count * capacity,), jnp.int32).at[dest_index].set(row_ids)
    gate_local = w_gate[0]
    up_local = w_up[0]
    down_local = w_down[0]
    projected = lax.psum(partial_value, "tp")
    own_part = lax.dynamic_slice_in_dim(projected, tp_index * part_width, part_width, 1)
    outgoing = projected.astype(jnp.bfloat16)[source_row].reshape(slot_count, capacity, full_width)
    incoming = lax.all_to_all(outgoing, "req", split_axis=0, concat_axis=0, tiled=True)
    expert_rows = incoming.reshape(slot_count * capacity, full_width)
    gate_act = jnp.dot(expert_rows, gate_local, preferred_element_type=jnp.float32)
    up_act = jnp.dot(expert_rows, up_local, preferred_element_type=jnp.float32)
    hidden = (jax.nn.silu(gate_act) * up_act).astype(jnp.bfloat16)
    expert_out = jnp.dot(
        lax.all_gather(hidden, "tp", axis=1, tiled=True),
        down_local,
        preferred_element_type=jnp.float32,
    )
    expert_out = expert_out.astype(jnp.bfloat16).reshape(slot_count, capacity, down_local.shape[1])
    returned = lax.all_to_all(expert_out, "req", split_axis=0, concat_axis=0, tiled=True)
    picked = returned.reshape(slot_count * capacity, part_width)[dest_index]
    picked = picked.reshape(row_count, route_count, part_width).astype(jnp.float32)
    routed_sum = jnp.sum(picked * gates[:, :, None], axis=1)
    combined = own_part + routed_sum
    square_part = jnp.sum(combined * combined, axis=1)
    square_total = lax.psum(square_part, "tp")
    scale = lax.rsqrt(square_total / full_width + 1e-06)
    return (combined * scale[:, None] * norm_gain[None, :]).astype(jnp.bfloat16)


def solution(mesh):
    placed = (
        P("req", "tp"),
        P("tp", None),
        P("req", "tp"),
        P("req", None),
        P("req", None),
        P("req", None, "tp"),
        P("req", None, "tp"),
        P("req", None, "tp"),
        P("tp"),
    )
    return jax.shard_map(
        body, mesh=mesh, in_specs=placed, out_specs=P("req", "tp"), check_vma=False
    )
```

profile of v0, /device:TPU:8, one launch (start us, length us, event | category | flops | bytes accessed | tf_op | source)
XLA Modules:
  0.0 315.9 jit_solution(1539475655118343820)
XLA Ops:
  6.5 1.6 copy-done
  8.1 1.3 fusion.12
  9.4 0.9 add_dynamic-update-slice_fusion
  10.3 0.8 copy-done.2
  11.3 0.1 eq.29
  11.4 0.1 eq.25
  11.6 0.1 copy.14
  11.7 0.2 fusion.5
  12.1 0.1 mul.61
  12.3 0.1 reshape.96
  12.4 0.2 fusion.7
  12.7 2.9 scatter_custom_fusion
  15.6 53.9 %all-reduce.2.cloned.1.call-done = f32[64,2048]{1,0:T(8,128)} async-done(((f32[64,2048]{1,0:T(8,128)}), f32[64,2048]{1,0:T(8,128)}) %all-reduce.2.cloned.1.call-update) | async-done | bytes 524304 | tf_op jit(solution)/shard_map/psum | solution.py:31
  69.5 1.1 convert_element_type.27
  70.6 4.3 %gather_fusion = bf16[768,2048]{1,0:T(8,128)(2,1)} fusion(bf16[64,2048]{1,0:T(8,128)(2,1)S(1)} %convert_element_type.27, s32[1024]{0:T(1024)S(1)} %pad_clamp_fusion.1), kind=kCustom, calls=%fused_computation | custom fusion | bytes 6294528 | tf_op jit(solution)/shard_map/gather | solution.py:33
  74.9 6.3 %reshape.71 = bf16[128,6,2048]{2,1,0:T(8,128)(2,1)} reshape(bf16[768,2048]{1,0:T(8,128)(2,1)} %gather_fusion) | data formatting | bytes 6291456 | tf_op jit(solution)/shard_map/reshape | solution.py:33
  81.1 111.0 %all_to_all.10 = bf16[128,6,2048]{2,1,0:T(8,128)(2,1)} all-to-all(bf16[128,6,2048]{2,1,0:T(8,128)(2,1)} %reshape.71), channel_id=1, replica_groups=mesh['req'=128,'tp'=4] {'req'}, dimensions={0} | all-to-all | bytes 6291456 | tf_op jit(solution)/shard_map/all_to_all | solution.py:34
  192.1 6.3 %reshape.72 = bf16[768,2048]{1,0:T(8,128)(2,1)} reshape(bf16[128,6,2048]{2,1,0:T(8,128)(2,1)} %all_to_all.10) | data formatting | bytes 6291456 | tf_op jit(solution)/shard_map/reshape | solution.py:35
  198.4 3.3 %fusion.3 = f32[768,256]{1,0:T(8,128)S(1)} fusion(bf16[768,2048]{1,0:T(8,128)(2,1)} %reshape.72, bf16[1,2048,256]{2,1,0:T(8,128)(2,1)} %param.14), kind=kOutput, calls=%fused_computation.8 | convolution fusion | flops 805306368 | bytes 4980736 | tf_op jit(solution)/shard_map/dot_general | solution.py:36
  201.9 1.7 fusion
  203.6 38.7 %all-gather.2.cloned.1.call-done = bf16[768,1024]{1,0:T(8,128)(2,1)} async-done(((bf16[768,256]{1,0:T(8,128)(2,1)}), bf16[768,1024]{1,0:T(8,128)(2,1)}) %all-gather.2.cloned.1.call-update) | async-done | bytes 1572880 | tf_op jit(solution)/shard_map/all_gather | solution.py:40
  242.3 2.7 convolution_convert_fusion
  245.0 1.3 reshape.73
  246.3 14.6 %all-to-all-start.1 = ((bf16[128,6,512]{2,1,0:T(8,128)(2,1)}), bf16[128,6,512]{2,1,0:T(8,128)(2,1)}, u32[]{:S(2)}, u32[]{:S(2)}) async-start(bf16[128,6,512]{2,1,0:T(8,128)(2,1)} %reshape.73), calls=%async_computation.1 | async-start | bytes 2097152 | tf_op jit(solution)/shard_map/all_to_all | solution.py:45
  260.9 0.7 copy.16
  261.6 30.2 %all-to-all-done.1 = bf16[128,6,512]{2,1,0:T(8,128)(2,1)} async-done(((bf16[128,6,512]{2,1,0:T(8,128)(2,1)}), bf16[128,6,512]{2,1,0:T(8,128)(2,1)}, u32[]{:S(2)}, u32[]{:S(2)}) %all-to-all-start.1) | async-done | bytes 786464 | tf_op jit(solution)/shard_map/all_to_all | solution.py:45
  291.9 1.4 reshape.74
  293.3 2.1 gather_fusion.1
  295.4 1.1 multiply_reduce_fusion
  296.6 1.0 multiply_reduce_fusion.1
  297.6 9.8 %psum.15 = f32[64]{0:T(128)S(1)} all-reduce(f32[64]{0:T(128)S(1)} %multiply_reduce_fusion.1), channel_id=1, replica_groups=mesh['req'=128,'tp'=4] {'tp'}, use_global_device_ids=true, to_apply=%region_7.8 | all-reduce | flops 64 | bytes 512 | tf_op jit(solution)/shard_map/psum | solution.py:51
  307.4 1.6 multiply_convert_fusion
  (30 shorter events, 0.7 us)
Async XLA Ops:
  6.5 1.6 copy-start
  6.5 4.6 %copy-start.3 = (s32[64,6]{0,1:T(8,128)S(1)}, s32[64,6]{0,1:T(8,128)}, u32[]{:S(2)}) copy-start(s32[64,6]{0,1:T(8,128)} %param.12) | copy-start | bytes 4612
  6.5 63.0 %all-reduce.2.cloned.1.call-start = ((), (), s32[]{:S(2)}) async-start(), calls=%async_computation.2 | async-start | bytes 1048576 | tf_op jit(solution)/shard_map/psum | solution.py:31
  10.3 0.8 copy-start.2
  11.1 231.1 %all-gather.2.cloned.1.call-start = ((), (), s32[]{:S(2)}) async-start(), calls=%async_computation.3 | async-start | bytes 1966080 | tf_op jit(solution)/shard_map/all_gather | solution.py:40
  198.4 3.3 %copy-start.1 = (bf16[768,2048]{1,0:T(8,128)(2,1)S(1)}, bf16[768,2048]{1,0:T(8,128)(2,1)}, u32[]{:S(2)}) copy-start(bf16[768,2048]{1,0:T(8,128)(2,1)} %reshape.72) | copy-start | bytes 9437188
  198.4 3.4 %copy-start.6 = (bf16[1,2048,256]{2,1,0:T(8,128)(2,1)S(1)}, bf16[1,2048,256]{2,1,0:T(8,128)(2,1)}, u32[]{:S(2)}) copy-start(bf16[1,2048,256]{2,1,0:T(8,128)(2,1)} %param.15) | copy-start | bytes 3145732
  245.0 15.9 %copy-start.4 = (f32[64,6]{0,1:T(8,128)S(1)}, f32[64,6]{0,1:T(8,128)}, u32[]{:S(2)}) copy-start(f32[64,6]{0,1:T(8,128)} %param.13) | copy-start | bytes 4612
  246.3 45.6 %all-to-all-start.1 = ((bf16[128,6,512]{2,1,0:T(8,128)(2,1)}), bf16[128,6,512]{2,1,0:T(8,128)(2,1)}, u32[]{:S(2)}, u32[]{:S(2)}) async-start(bf16[128,6,512]{2,1,0:T(8,128)(2,1)} %reshape.73), calls=%async_computation.1 | async-start | bytes 2097152 | tf_op jit(solution)/shard_map/all_to_all | solution.py:45
  293.2 14.2 %copy-start.5 = (f32[512]{0:T(512)S(1)}, f32[512]{0:T(512)}, u32[]{:S(2)}) copy-start(f32[512]{0:T(512)} %param.17) | copy-start | bytes 6148
Sparse Core Ops, SparseCore 0:
  11.3 58.2 all-reduce.1
  203.7 38.5 all-gather.1
where the time goes:
time: 317 us; the launch traced here: 316 us
  waiting for transfers between devices  123 us (39%)
  blocking collectives  121 us (38%)
  local copies, waits for them, and re-layouts  28.7 us (9%)
  starting transfers between devices  14.7 us (5%)
  between operations  13.6 us (4%)
  matrix products  9.02 us (3%)
  other arithmetic  6.31 us (2%)
    all_to_all x1, blocking collectives, body(): lax.all_to_all(outgoing, 'req', split_axis=0, concat_axis=0, tiled=True)  111 us
    psum x1, waiting for transfers between devices, body(): projected = lax.psum(partial_value, 'tp')  53.9 us
    all_gather x1, waiting for transfers between devices, body(): lax.all_gather(hidden, 'tp', axis=1, tiled=True)  38.7 us
    all_to_all x1, waiting for transfers between devices, body(): lax.all_to_all(expert_out, 'req', split_axis=0, concat_axis=0, tiled=True)  30.2 us
    all_to_all x1, starting transfers between devices, body(): lax.all_to_all(expert_out, 'req', split_axis=0, concat_axis=0, tiled=True)  14.6 us
    psum x1, blocking collectives, body(): square_total = lax.psum(square_part, 'tp')  9.8 us
  transfers between devices with their start and end apart: 3, of which 3 were waited for; matrix products, arithmetic and copies ran while one was open for 2% of the time, Pallas kernels for 0%

commit v1 on v0

--- a/solution.py
+++ b/solution.py
@@ -2,6 +2,24 @@
 import jax.numpy as jnp
 from jax import lax
 from jax.sharding import PartitionSpec as P
+
+
+def gather_around(shard, axis, dim):
+    ways, here, lap = (lax.axis_size(axis), lax.axis_index(axis), shard.shape[dim])
+    lengths = [n * ways if d == dim else n for d, n in enumerate(shard.shape)]
+    full = lax.dynamic_update_slice_in_dim(
+        jnp.zeros(lengths, shard.dtype), shard, here * lap, axis=dim
+    )
+    going_up = going_down = shard
+    for far in range(1, ways // 2 + 1):
+        going_up = lax.ppermute(going_up, axis, [(d, (d + 1) % ways) for d in range(ways)])
+        full = lax.dynamic_update_slice_in_dim(full, going_up, (here - far) % ways * lap, axis=dim)
+        if 2 * far < ways:
+            going_down = lax.ppermute(going_down, axis, [(d, (d - 1) % ways) for d in range(ways)])
+            full = lax.dynamic_update_slice_in_dim(
+                full, going_down, (here + far) % ways * lap, axis=dim
+            )
+    return full
 
 
 def body(attn_out, w_out, residual, routes, gates, w_gate, w_up, w_down, norm_gain):
@@ -37,9 +55,7 @@
     up_act = jnp.dot(expert_rows, up_local, preferred_element_type=jnp.float32)
     hidden = (jax.nn.silu(gate_act) * up_act).astype(jnp.bfloat16)
     expert_out = jnp.dot(
-        lax.all_gather(hidden, "tp", axis=1, tiled=True),
-        down_local,
-        preferred_element_type=jnp.float32,
+        gather_around(hidden, "tp", 1), down_local, preferred_element_type=jnp.float32
     )
     expert_out = expert_out.astype(jnp.bfloat16).reshape(slot_count, capacity, down_local.shape[1])
     returned = lax.all_to_all(expert_out, "req", split_axis=0, concat_axis=0, tiled=True)

time: 317 us -> 307 us (0.968)
  the two profiles are of different devices: /device:TPU:8 before, /device:TPU:10 now
where the time goes in v1:
time: 307 us; the launch traced here: 306 us
  waiting for transfers between devices  192 us (63%)
  starting transfers between devices  43.5 us (14%)
  local copies, waits for them, and re-layouts  32.4 us (11%)
  between operations  13.7 us (4%)
  blocking collectives  10.7 us (3%)
  matrix products  8.47 us (3%)
  other arithmetic  5.47 us (2%)
    all_to_all x1, waiting for transfers between devices, body(): lax.all_to_all(outgoing, 'req', split_axis=0, concat_axis=0, tiled=True)  96.3 us
    psum x1, waiting for transfers between devices, body(): projected = lax.psum(partial_value, 'tp')  53 us
    all_to_all x1, waiting for transfers between devices, body(): lax.all_to_all(expert_out, 'req', split_axis=0, concat_axis=0, tiled=True)  30.2 us
    all_to_all x1, starting transfers between devices, body(): lax.all_to_all(expert_out, 'req', split_axis=0, concat_axis=0, tiled=True)  19.3 us
    all_to_all x1, starting transfers between devices, body(): lax.all_to_all(outgoing, 'req', split_axis=0, concat_axis=0, tiled=True)  14.6 us
    ppermute x2, waiting for transfers between devices, gather_around(): lax.ppermute(going_up, axis, [(d, (d + 1) % ways) for d in range(ways)])  12.3 us
    psum x1, blocking collectives, body(): square_total = lax.psum(square_part, 'tp')  10.7 us
    ppermute x2, starting transfers between devices, gather_around(): lax.ppermute(going_up, axis, [(d, (d + 1) % ways) for d in range(ways)])  7.41 us
  transfers between devices with their start and end apart: 6, of which 5 were waited for; matrix products, arithmetic and copies ran while one was open for 2% of the time, Pallas kernels for 0%

profile of v1, /device:TPU:10, one launch (start us, length us, event | category | flops | bytes accessed | tf_op | source)
XLA Modules:
  0.0 306.1 jit_solution(10488028393315566425)
XLA Ops:
  6.6 1.6 copy-done
  8.1 1.3 fusion.12
  9.5 0.8 copy-done.2
  11.8 2.9 scatter_custom_fusion
  14.8 53.0 %all-reduce.2.cloned.1.call-done = f32[64,2048]{1,0:T(8,128)} async-done(((f32[64,2048]{1,0:T(8,128)}), f32[64,2048]{1,0:T(8,128)}) %all-reduce.2.cloned.1.call-update) | async-done | bytes 524304 | tf_op jit(solution)/shard_map/psum | solution.py:49
  67.7 1.1 convert_element_type.27
  68.8 4.3 %gather_fusion = bf16[768,2048]{1,0:T(8,128)(2,1)} fusion(bf16[64,2048]{1,0:T(8,128)(2,1)S(1)} %convert_element_type.27, s32[1024]{0:T(1024)S(1)} %pad_clamp_fusion.1), kind=kCustom, calls=%fused_computation | custom fusion | bytes 6294528 | tf_op jit(solution)/shard_map/gather | solution.py:51
  73.1 6.3 %reshape.71 = bf16[128,6,2048]{2,1,0:T(8,128)(2,1)} reshape(bf16[768,2048]{1,0:T(8,128)(2,1)} %gather_fusion) | data formatting | bytes 6291456 | tf_op jit(solution)/shard_map/reshape | solution.py:51
  79.3 14.6 %all-to-all-start = ((bf16[128,6,2048]{2,1,0:T(8,128)(2,1)}), bf16[128,6,2048]{2,1,0:T(8,128)(2,1)}, u32[]{:S(2)}, u32[]{:S(2)}) async-start(bf16[128,6,2048]{2,1,0:T(8,128)(2,1)} %reshape.71), calls=%async_computation | async-start | bytes 8388608 | tf_op jit(solution)/shard_map/all_to_all | solution.py:52
  94.0 96.3 %all-to-all-done = bf16[128,6,2048]{2,1,0:T(8,128)(2,1)} async-done(((bf16[128,6,2048]{2,1,0:T(8,128)(2,1)}), bf16[128,6,2048]{2,1,0:T(8,128)(2,1)}, u32[]{:S(2)}, u32[]{:S(2)}) %all-to-all-start) | async-done | bytes 3145760 | tf_op jit(solution)/shard_map/all_to_all | solution.py:52
  190.3 6.3 %reshape.72 = bf16[768,2048]{1,0:T(8,128)(2,1)} reshape(bf16[128,6,2048]{2,1,0:T(8,128)(2,1)} %all-to-all-done) | data formatting | bytes 6291456 | tf_op jit(solution)/shard_map/reshape | solution.py:53
  196.6 3.0 fusion.3
  199.9 1.7 constant_dynamic-update-slice_fusion.2
  201.6 1.2 copy-done.3
  202.8 3.7 %collective-permute-start = (bf16[768,256]{1,0:T(8,128)(2,1)}, bf16[768,256]{1,0:T(8,128)(2,1)S(1)}, u32[]{:S(2)}, u32[]{:S(2)}) collective-permute-start(bf16[768,256]{1,0:T(8,128)(2,1)} %get-tuple-element.6), channel_id=1, source_target_pairs={{0,1},{1,2},{2,3},{3,0},{4,5},{5,6},{6,7},{7,4},{8,9},{9,10},{10,1... | collective-permute-start | bytes 1179656 | tf_op jit(solution)/shard_map/ppermute | solution.py:15
  206.5 2.1 collective-permute-start.1
  208.6 6.0 %collective-permute-done = bf16[768,256]{1,0:T(8,128)(2,1)S(1)} collective-permute-done((bf16[768,256]{1,0:T(8,128)(2,1)}, bf16[768,256]{1,0:T(8,128)(2,1)S(1)}, u32[]{:S(2)}, u32[]{:S(2)}) %collective-permute-start) | collective-permute-done | bytes 393248 | tf_op jit(solution)/shard_map/ppermute | solution.py:15
  214.7 3.7 %collective-permute-start.2 = (bf16[768,256]{1,0:T(8,128)(2,1)S(1)}, bf16[768,256]{1,0:T(8,128)(2,1)S(1)}, u32[]{:S(2)}, u32[]{:S(2)}) collective-permute-start(bf16[768,256]{1,0:T(8,128)(2,1)S(1)} %collective-permute-done), channel_id=1, source_target_pairs={{0,1},{1,2},{2,3},{3,0},{4,5},{5,6},{6,7},{7,4},{8,9},{9,10},{10,1... | collective-permute-start | bytes 1179656 | tf_op jit(solution)/shard_map/ppermute | solution.py:15
  218.4 0.8 constant_dynamic-update-slice_fusion.1
  219.3 0.8 constant_dynamic-update-slice_fusion
  220.1 6.3 %collective-permute-done.2 = bf16[768,256]{1,0:T(8,128)(2,1)S(1)} collective-permute-done((bf16[768,256]{1,0:T(8,128)(2,1)S(1)}, bf16[768,256]{1,0:T(8,128)(2,1)S(1)}, u32[]{:S(2)}, u32[]{:S(2)}) %collective-permute-start.2) | collective-permute-done | bytes 393248 | tf_op jit(solution)/shard_map/ppermute | solution.py:15
  226.4 0.8 constant_dynamic-update-slice_fusion.3
  227.2 2.4 convolution_convert_fusion
  229.6 1.3 reshape.73
  230.9 19.3 %all-to-all-start.1 = ((bf16[128,6,512]{2,1,0:T(8,128)(2,1)}), bf16[128,6,512]{2,1,0:T(8,128)(2,1)}, u32[]{:S(2)}, u32[]{:S(2)}) async-start(bf16[128,6,512]{2,1,0:T(8,128)(2,1)} %reshape.73), calls=%async_computation.1 | async-start | bytes 2097152 | tf_op jit(solution)/shard_map/all_to_all | solution.py:61
  250.9 30.2 %all-to-all-done.1 = bf16[128,6,512]{2,1,0:T(8,128)(2,1)} async-done(((bf16[128,6,512]{2,1,0:T(8,128)(2,1)}), bf16[128,6,512]{2,1,0:T(8,128)(2,1)}, u32[]{:S(2)}, u32[]{:S(2)}) %all-to-all-start.1) | async-done | bytes 786464 | tf_op jit(solution)/shard_map/all_to_all | solution.py:61
  281.1 1.4 reshape.74
  282.5 2.1 gather_fusion.1
  284.7 1.1 multiply_reduce_fusion
  285.9 1.0 multiply_reduce_fusion.1
  286.9 10.7 %psum.15 = f32[64]{0:T(128)S(1)} all-reduce(f32[64]{0:T(128)S(1)} %multiply_reduce_fusion.1), channel_id=1, replica_groups=mesh['req'=128,'tp'=4] {'tp'}, use_global_device_ids=true, to_apply=%region_7.8 | all-reduce | flops 64 | bytes 512 | tf_op jit(solution)/shard_map/psum | solution.py:67
  297.6 1.6 multiply_convert_fusion
  (46 shorter events, 2.5 us)
Async XLA Ops:
  6.5 1.6 copy-start
  6.5 2.9 copy-start.4
  6.5 3.8 %copy-start.5 = (s32[64,6]{0,1:T(8,128)S(1)}, s32[64,6]{0,1:T(8,128)}, u32[]{:S(2)}) copy-start(s32[64,6]{0,1:T(8,128)} %param.12) | copy-start | bytes 4612
  6.5 61.2 %all-reduce.2.cloned.1.call-start = ((), (), s32[]{:S(2)}) async-start(), calls=%async_computation.2 | async-start | bytes 1048576 | tf_op jit(solution)/shard_map/psum | solution.py:49
  9.5 0.8 copy-start.2
  79.3 111.0 %all-to-all-start = ((bf16[128,6,2048]{2,1,0:T(8,128)(2,1)}), bf16[128,6,2048]{2,1,0:T(8,128)(2,1)}, u32[]{:S(2)}, u32[]{:S(2)}) async-start(bf16[128,6,2048]{2,1,0:T(8,128)(2,1)} %reshape.71), calls=%async_computation | async-start | bytes 8388608 | tf_op jit(solution)/shard_map/all_to_all | solution.py:52
  94.0 102.7 %copy-start.8 = (bf16[1,2048,256]{2,1,0:T(8,128)(2,1)S(1)}, bf16[1,2048,256]{2,1,0:T(8,128)(2,1)}, u32[]{:S(2)}) copy-start(bf16[1,2048,256]{2,1,0:T(8,128)(2,1)} %param.14) | copy-start | bytes 3145732
  196.6 3.2 %copy-start.1 = (bf16[768,2048]{1,0:T(8,128)(2,1)S(1)}, bf16[768,2048]{1,0:T(8,128)(2,1)}, u32[]{:S(2)}) copy-start(bf16[768,2048]{1,0:T(8,128)(2,1)} %reshape.72) | copy-start | bytes 9437188
  196.6 3.2 %copy-start.9 = (bf16[1,2048,256]{2,1,0:T(8,128)(2,1)S(1)}, bf16[1,2048,256]{2,1,0:T(8,128)(2,1)}, u32[]{:S(2)}) copy-start(bf16[1,2048,256]{2,1,0:T(8,128)(2,1)} %param.15) | copy-start | bytes 3145732
  201.6 1.2 copy-start.3
  202.8 11.9 %collective-permute-start = (bf16[768,256]{1,0:T(8,128)(2,1)}, bf16[768,256]{1,0:T(8,128)(2,1)S(1)}, u32[]{:S(2)}, u32[]{:S(2)}) collective-permute-start(bf16[768,256]{1,0:T(8,128)(2,1)} %get-tuple-element.6), channel_id=1, source_target_pairs={{0,1},{1,2},{2,3},{3,0},{4,5},{5,6},{6,7},{7,4},{8,9},{9,10},{10,1... | collective-permute-start | bytes 1179656 | tf_op jit(solution)/shard_map/ppermute | solution.py:15
  206.5 12.8 %collective-permute-start.1 = (bf16[768,256]{1,0:T(8,128)(2,1)}, bf16[768,256]{1,0:T(8,128)(2,1)S(1)}, u32[]{:S(2)}, u32[]{:S(2)}) collective-permute-start(bf16[768,256]{1,0:T(8,128)(2,1)} %get-tuple-element.6), channel_id=1, source_target_pairs={{0,3},{1,0},{2,1},{3,2},{4,7},{5,4},{6,5},{7,6},{8,11},{9,8},{10,9... | collective-permute-start | bytes 1179656 | tf_op jit(solution)/shard_map/ppermute | solution.py:18
  214.7 11.7 %collective-permute-start.2 = (bf16[768,256]{1,0:T(8,128)(2,1)S(1)}, bf16[768,256]{1,0:T(8,128)(2,1)S(1)}, u32[]{:S(2)}, u32[]{:S(2)}) collective-permute-start(bf16[768,256]{1,0:T(8,128)(2,1)S(1)} %collective-permute-done), channel_id=1, source_target_pairs={{0,1},{1,2},{2,3},{3,0},{4,5},{5,6},{6,7},{7,4},{8,9},{9,10},{10,1... | collective-permute-start | bytes 1179656 | tf_op jit(solution)/shard_map/ppermute | solution.py:15
  218.4 8.7 %copy-start.10 = (bf16[1,1024,512]{2,1,0:T(8,128)(2,1)S(1)}, bf16[1,1024,512]{2,1,0:T(8,128)(2,1)}, u32[]{:S(2)}) copy-start(bf16[1,1024,512]{2,1,0:T(8,128)(2,1)} %param.16) | copy-start | bytes 3145732
  229.6 20.6 %copy-start.6 = (f32[64,6]{0,1:T(8,128)S(1)}, f32[64,6]{0,1:T(8,128)}, u32[]{:S(2)}) copy-start(f32[64,6]{0,1:T(8,128)} %param.13) | copy-start | bytes 4612
  230.9 50.3 %all-to-all-start.1 = ((bf16[128,6,512]{2,1,0:T(8,128)(2,1)}), bf16[128,6,512]{2,1,0:T(8,128)(2,1)}, u32[]{:S(2)}, u32[]{:S(2)}) async-start(bf16[128,6,512]{2,1,0:T(8,128)(2,1)} %reshape.73), calls=%async_computation.1 | async-start | bytes 2097152 | tf_op jit(solution)/shard_map/all_to_all | solution.py:61
  284.6 13.0 %copy-start.7 = (f32[512]{0:T(512)S(1)}, f32[512]{0:T(512)}, u32[]{:S(2)}) copy-start(f32[512]{0:T(512)} %param.17) | copy-start | bytes 6148
Sparse Core Ops, SparseCore 0:
  10.4 57.2 all-reduce.1
